TPU v7x, 32 devices: a whole 2x2x4 slice. The times are simulated.
32 devices in a mesh: wave: 4 (over z), tile: 8 (over y, x, core).
Axes of the slice: x: 2, y: 2, z: 4, core: 2. Of those that a mesh axis runs over, the one named last changes fastest.
Arguments:
- spectral: bfloat16 [640, 2, 64, 1281], P('wave', None, 'tile'), may hold values from -0.083496094 to 0.083496094
- legendre: bfloat16 [640, 8, 1281], P('wave'), may hold values from -0.25 to 0.25
- pair_ids: int32 [640], replicated, may hold values from 0 to 639, each once
Outputs:
- spectral_out: bfloat16 [640, 2, 64, 1281], P('wave', None, 'tile')
Inputs may be any that keep to these rules, and one draw needn't show every extreme that they name: A permutation: each pair 0 to 639 appears once; slot s of spectral, legendre and spectral_out holds wavenumbers pair_ids[s] and 1279 - pair_ids[s].
All inputs are finite; a program needn't handle non-finite values.
Results may differ from a plain program's by a relative error of at most 0.0072.
Values may be sent and summed in bfloat16 or wider, within the bound.
A program may use at most 64 MiB of HBM per device.

v0:
```python
import functools
import math
import jax
import jax.numpy as jnp
from jax import lax
from jax.sharding import PartitionSpec as P

MW = 1280
HALF_LATS = 1280
PAIRS = 640
NPTS = 5156
LANES = 128
RADIX = 32
F32 = jnp.float32
BF16 = jnp.bfloat16


def cycle_lengths(pair_number, pair_total):
    polar_cycle = pair_number * (HALF_LATS // 2) // pair_total
    cycle_index = jnp.stack([polar_cycle, HALF_LATS - 1 - polar_cycle])
    return (cycle_index, 20 + 4 * cycle_index)


def cycle_scale(cycle_index, cycle_len, lat_count):
    angles = math.pi * (cycle_index.astype(F32) + 0.5) / (2.0 * HALF_LATS)
    return 40.0 * jnp.sin(angles) / jnp.sqrt(lat_count * cycle_len.astype(F32))


def trig(wavenumbers, local_index, length):
    phase = wavenumbers[:, None] * local_index[None, :] % length[None, :]
    angles = 2.0 * math.pi * phase.astype(F32) / length[None, :].astype(F32)
    return (jnp.cos(angles), jnp.sin(angles))


def tables(local_index, length):
    outer = MW // 2 // RADIX
    a_cos, a_sin = trig(2 * RADIX * lax.iota(jnp.int32, outer), local_index, length)
    b_cos, b_sin = trig(lax.iota(jnp.int32, 2 * RADIX), local_index, length)
    pts = local_index.shape[0]
    b_cos = b_cos.reshape(RADIX, 2, pts).transpose(1, 0, 2)[:, None]
    b_sin = b_sin.reshape(RADIX, 2, pts).transpose(1, 0, 2)[:, None]
    a_cos, a_sin = (a_cos[None, :, None], a_sin[None, :, None])
    cos = (a_cos * b_cos - a_sin * b_sin).astype(BF16).reshape(2, MW // 2, pts)
    sin = (a_sin * b_cos + a_cos * b_sin).astype(BF16).reshape(2, MW // 2, pts)
    return (cos, sin)


def grid_products(grid_values):
    layer_count = grid_values.shape[0] // 4
    u, w, t, q = grid_values.astype(F32).reshape(4, layer_count, grid_values.shape[1])
    level = lax.iota(jnp.int32, layer_count)
    acc, rows = (t[layer_count - 1], [])
    rows.append(acc)
    for v in range(layer_count - 2, -1, -1):
        acc = acc + t[v]
        rows.append(acc)
    geo = jnp.stack(rows[::-1]) / math.sqrt(layer_count)
    energy = 0.5 * (u * u + w * w) + geo
    return jnp.stack([energy, u * t, w * t, u * q]).reshape(grid_values.shape).astype(BF16)


def local(spectral, legendre, pair_ids):
    slots, _, cols, row_total = spectral.shape
    lat_count = legendre.shape[1]
    tiles = lax.axis_size("tile")
    zero = jnp.zeros((), BF16)
    wave_here = lax.axis_index("wave")
    slot_ids = lax.dynamic_slice_in_dim(pair_ids, wave_here * slots, slots)
    row_index = lax.broadcasted_iota(jnp.int32, (slots, row_total), 1)
    upper = (row_index >= (MW - slot_ids)[:, None])[:, None, :]
    masked = jnp.concatenate(
        [jnp.where(upper, zero, legendre), jnp.where(upper, legendre, zero)], axis=1
    )
    spec = spectral.reshape(slots, 2 * cols, row_total)
    cycle_index, cycle_len = cycle_lengths(wave_here, lat_count // 2)
    scales = cycle_scale(cycle_index, cycle_len, lat_count)
    quarter = NPTS // 4
    step = (
        tiles * LANES // math.gcd(4, tiles) if tiles * LANES // math.gcd(4, tiles) <= 512 else 512
    )
    kpad = -(-quarter // step) * step
    k = lax.iota(jnp.int32, kpad)
    q0 = cycle_len[0] // 4
    second = k >= q0
    inside = k < quarter
    local_index = jnp.where(inside, k - jnp.where(second, q0, 0), 0)
    length = jnp.where(second, cycle_len[1], cycle_len[0])
    cos, sin = tables(local_index, length)
    half = MW // 2
    m_order = jnp.arange(MW, dtype=jnp.int32).reshape(half, 2).T
    quarter_m = half // 2
    m0, m1 = (m_order[:, :quarter_m], m_order[:, quarter_m:])
    q_of = jnp.stack([m0, MW - 1 - m1]).reshape(2, half)
    hot = (pair_ids[None, :, None] == q_of[:, None, :]).astype(BF16)
    coefficients = (
        lax.dot_general(masked, spec, (((2,), (2,)), ((0,), (0,))), preferred_element_type=F32)
        .astype(BF16)
        .reshape(slots, 2, lat_count, 2 * cols)
    )
    coefficients = coefficients.transpose(2, 1, 3, 0)
    fourier = lax.all_to_all(coefficients, "wave", split_axis=0, concat_axis=3, tiled=True)
    ordered = lax.dot_general(
        fourier, hot, (((3,), (1,)), ((1,), (0,))), preferred_element_type=F32
    )
    ordered = ordered.reshape(2, 2, 2, cols, 2, quarter_m).transpose(4, 2, 1, 3, 0, 5)
    ordered = ordered.reshape(2, 2, 2, cols, half)
    factor = jnp.where(m_order == 0, 1.0, 2.0).astype(F32)
    keep = 2 * m_order[:, None, :] < cycle_len[None, :, None]
    ordered = ordered * jnp.where(keep, factor[:, None, :], 0.0)[:, None, :, None, :]
    sign = jnp.where(m_order // 2 % 2 == 0, 1.0, -1.0).astype(F32)
    re, im = (ordered[:, 0].reshape(2, 2 * cols, half), ordered[:, 1].reshape(2, 2 * cols, half))
    even_c = jnp.concatenate([re[0], re[0] * sign[0]]).astype(BF16)
    even_s = jnp.concatenate([-im[0], -im[0] * sign[0]]).astype(BF16)
    odd_c = jnp.concatenate([re[1], im[1] * sign[1]]).astype(BF16)
    odd_s = jnp.concatenate([-im[1], re[1] * sign[1]]).astype(BF16)
    dot = functools.partial(jnp.dot, preferred_element_type=F32)
    even = (dot(even_c, cos[0]) + dot(even_s, sin[0])).reshape(2, 2, cols, kpad)
    odd = (dot(odd_c, cos[1]) + dot(odd_s, sin[1])).reshape(2, 2, cols, kpad)
    even = jnp.where(second, even[:, 1], even[:, 0])
    odd = jnp.where(second, odd[:, 1], odd[:, 0])
    grid_values = jnp.stack(
        [even[0] + odd[0], even[1] - odd[1], even[0] - odd[0], even[1] + odd[1]], axis=1
    ).astype(BF16)
    grid_values = grid_values.reshape(cols, 4 * kpad)
    grid_values = lax.all_to_all(grid_values, "tile", split_axis=1, concat_axis=0, tiled=True)
    product = grid_products(grid_values)
    product = lax.all_to_all(product, "tile", split_axis=0, concat_axis=1, tiled=True)
    x = product.astype(F32).reshape(cols, 4, kpad)
    x = jnp.where(inside, x, 0.0)
    x0, x1, x2, x3 = (x[:, 0], x[:, 1], x[:, 2], x[:, 3])

    def by_lat(a, b):
        both = jnp.stack([a, b])[:, None]
        return (
            jnp.where(second == (lax.iota(jnp.int32, 2) == 1)[None, :, None, None], both, 0.0)
            .astype(BF16)
            .reshape(4 * cols, kpad)
        )

    even_in = by_lat(x0 + x2 + (x1 + x3), x0 + x2 - (x1 + x3))
    odd_in = by_lat(x0 - x2, x1 - x3)
    nt = lambda a, b: lax.dot_general(
        a, b, (((1,), (1,)), ((), ())), preferred_element_type=F32
    ).reshape(2, 2, cols, half)
    ec, es = (nt(even_in, cos[0]), nt(even_in, sin[0]))
    oc, os_ = (nt(odd_in, cos[1]), nt(odd_in, sin[1]))
    pick = sign[0] > 0
    even_re = jnp.where(pick, ec[0], ec[1])
    even_im = -jnp.where(pick, es[0], es[1])
    odd_re = oc[0] - sign[1] * os_[1]
    odd_im = -os_[0] - sign[1] * oc[1]
    back = jnp.stack([jnp.stack([even_re, even_im]), jnp.stack([odd_re, odd_im])])
    back = back * jnp.where(keep, scales[None, :, None], 0.0)[:, None, :, None, :]
    back = back.astype(BF16).reshape(2, 2, 2, cols, 2, quarter_m).transpose(4, 2, 1, 3, 0, 5)
    back = back.reshape(2, 4 * cols, half)
    back = lax.dot_general(
        back, hot, (((2,), (2,)), ((0,), (0,))), preferred_element_type=F32
    ).astype(BF16)
    back = back.reshape(2, 2, 2 * cols, PAIRS).transpose(1, 0, 2, 3)
    returned = lax.all_to_all(back, "wave", split_axis=3, concat_axis=0, tiled=True)
    returned = returned.transpose(3, 2, 1, 0).reshape(slots, 2 * cols, 2 * lat_count)
    result = lax.dot_general(
        returned, masked, (((2,), (1,)), ((0,), (0,))), preferred_element_type=F32
    )
    return result.reshape(slots, 2, cols, row_total).astype(BF16)


def solution(mesh):
    placed = (P("wave", None, "tile", None), P("wave", None, None), P())
    return jax.shard_map(
        local, mesh=mesh, in_specs=placed, out_specs=P("wave", None, "tile", None), check_vma=False
    )
```

profile of v0, /device:TPU:0, one launch (start us, length us, event | category | flops | bytes accessed | tf_op | source)
XLA Modules:
  0.0 97.7 jit_solution(9886017591165895922)
XLA Ops:
  0.0 0.8 dynamic-slice_subtract_fusion
  0.8 0.2 iota_compare_fusion
  1.0 5.1 %broadcast_select_fusion.1 = (bf16[160,8,1281]{2,1,0:T(8,128)(2,1)}, bf16[160,8,1281]{2,1,0:T(8,128)(2,1)}) fusion(bf16[160,8,1281]{2,1,0:T(8,128)(2,1)} %param.4, pred[160,1281]{1,0:T(8,128)(4,1)S(1)} %iota_compare_fusion), kind=kLoop, calls=%fused_computation.10 | loop fusion | flops 3279360 | bytes 10043040 | tf_op jit(solution)/shard_map/jit(_where)/select_n | solution.py:72
  6.1 8.6 %fusion.12 = bf16[160,2,8,16]{3,2,1,0:T(8,128)(2,1)S(1)} fusion(bf16[160,2,8,1281]{3,2,1,0:T(8,128)(2,1)} %param.3, bf16[160,8,1281]{2,1,0:T(8,128)(2,1)} %get-tuple-element.27, bf16[160,8,1281]{2,1,0:T(8,128)(2,1)} %get-tuple-element.26), kind=kOutput, calls=%fused_computation.19 | convolution fusion | flops 118097920 | bytes 13199360 | tf_op jit(solution)/shard_map/dot_general | solution.py:96
  14.6 1.2 %copy.44 = bf16[160,2,8,16]{0,3,1,2:T(8,128)(2,1)} copy(bf16[160,2,8,16]{3,2,1,0:T(8,128)(2,1)S(1)} %fusion.12) | data formatting | bytes 163840 | tf_op jit(solution)/shard_map/reshape | solution.py:98
  15.9 6.3 %all-to-all-start = ((bf16[8,2,16,160]{3,2,1,0:T(8,128)(2,1)}), bf16[8,2,16,160]{3,2,1,0:T(8,128)(2,1)S(1)}, u32[]{:S(2)}, u32[]{:S(2)}) async-start(bf16[8,2,16,160]{3,2,1,0:T(8,128)(2,1)} %bitcast.5), calls=%async_computation | async-start | bytes 262144 | tf_op jit(solution)/shard_map/all_to_all | solution.py:101
  22.2 0.1 multiply_add_fusion.2
  22.3 0.1 rsqrt_multiply_fusion
  22.4 0.6 fusion.82
  25.6 1.3 %iota_compare_fusion.2 = (pred[1536]{0:T(1024)(128)(4,1)S(1)}, pred[1536]{0:T(1024)(128)(4,1)S(1)}) fusion(s32[]{:T(128)S(6)} %select_n.232, s32[]{:T(128)} %bitcast.2, s32[]{:T(128)} %bitcast.13), kind=kLoop, calls=%fused_computation.136 | loop fusion | flops 7680 | bytes 3084 | tf_op jit(solution)/shard_map/ge | solution.py:84
  26.9 1.3 %compare_select_fusion.1 = (s32[1536]{0:T(1024)S(1)}, f32[1536]{0:T(1024)S(1)}) fusion(s32[]{:T(128)} %bitcast.2, s32[]{:T(128)} %bitcast.13, s32[]{:T(128)S(6)} %select_n.232), kind=kLoop, calls=%fused_computation.123 | loop fusion | flops 7680 | bytes 12300 | tf_op jit(solution)/shard_map/jit(remainder)/jit(_where)/select_n | solution.py:30
  28.2 0.1 fusion.81
  28.3 2.1 %fusion.39 = (f32[20,1536]{1,0:T(8,128)S(1)}, f32[20,1536]{1,0:T(8,128)S(1)}) fusion(f32[1536]{0:T(1024)S(1)} %get-tuple-element.78, pred[1536]{0:T(1024)(128)(4,1)S(1)} %get-tuple-element.80, s32[1536]{0:T(1024)S(1)} %get-tuple-element.77, s32[1536]{0:T(1024)S(1)} %subtract_select_fusion, s32[20]{0:T(128)S(1)} %iota_multiply_fusion), kind=kLoop, calls=%fused_computation.65 | loop fusion | flops 337920 | bytes 265808 | tf_op jit(solution)/shard_map/cos | solution.py:32
  30.3 5.3 %fusion.27 = (f32[2,32,1536]{2,1,0:T(8,128)S(1)}, f32[2,32,1536]{2,1,0:T(8,128)S(1)}) fusion(f32[1536]{0:T(1024)S(1)} %get-tuple-element.78, pred[1536]{0:T(1024)(128)(4,1)S(1)} %get-tuple-element.80, s32[1536]{0:T(1024)S(1)} %get-tuple-element.77, s32[1536]{0:T(1024)S(1)} %subtract_select_fusion, s32[2,32]{1,0:T(2,128)S(1)} %multiply_add_fusion.1), kind=kLoop, calls=%fused_computation.40 | loop fusion | flops 1081344 | bytes 806656 | tf_op jit(solution)/shard_map/cos | solution.py:32
  35.6 2.5 %add_convert_fusion = (bf16[2,20,32,1536]{3,2,1,0:T(8,128)(2,1)S(1)}, bf16[2,20,32,1536]{3,2,1,0:T(8,128)(2,1)S(1)}) fusion(f32[2,32,1536]{2,1,0:T(8,128)S(1)} %get-tuple-element.62, f32[20,1536]{1,0:T(8,128)S(1)} %get-tuple-element.64, f32[2,32,1536]{2,1,0:T(8,128)S(1)} %get-tuple-element.61, f32[20,1536]{1,0:T(8,128)S(1)} %get-tuple-element.63), kind=kLoop, calls=%fused_computation | loop fusion | flops 15728640 | bytes 8896512 | tf_op jit(solution)/shard_map/convert_element_type | solution.py:44
  38.1 1.5 %fusion.75 = (bf16[1,20,32,1536]{3,2,1,0:T(8,128)(2,1)}, bf16[1,20,32,1536]{3,2,1,0:T(8,128)(2,1)S(1)}) fusion(bf16[2,20,32,1536]{3,2,1,0:T(8,128)(2,1)S(1)} %get-tuple-element.28), kind=kLoop, calls=%fused_computation.178 | loop fusion | bytes 7864320 | tf_op jit(solution)/shard_map/slice | solution.py:117
  39.6 2.3 %fusion.76 = (bf16[1,20,32,1536]{3,2,1,0:T(8,128)(2,1)}, bf16[1,20,32,1536]{3,2,1,0:T(8,128)(2,1)}) fusion(bf16[2,20,32,1536]{3,2,1,0:T(8,128)(2,1)S(1)} %get-tuple-element.29), kind=kLoop, calls=%fused_computation.179 | loop fusion | bytes 7864320 | tf_op jit(solution)/shard_map/slice | solution.py:117
  42.1 0.1 broadcast_compare_fusion
  42.2 0.1 mul.322
  42.2 0.1 stack.45
  42.3 0.1 stack.46
  42.4 0.1 copy.70
  42.5 0.1 all_to_all.45
  42.7 0.7 fusion.4
  43.4 0.2 reshape.906
  43.6 0.2 copy.68
  43.8 0.2 reshape.907
  44.0 2.1 %fusion.43 = f32[32,1536]{1,0:T(8,128)S(1)} fusion(bf16[640,1536]{1,0:T(8,128)(2,1)} %bitcast.174, bf16[16,640]{1,0:T(8,128)(2,1)S(1)} %get-tuple-element.43, bf16[16,640]{1,0:T(8,128)(2,1)S(1)} %get-tuple-element.49), kind=kOutput, calls=%fused_computation.92 | convolution fusion | flops 62996480 | bytes 2203648 | tf_op jit(solution)/shard_map/dot_general | solution.py:117
  46.1 2.0 %fusion.50 = f32[32,1536]{1,0:T(8,128)S(1)} fusion(bf16[640,1536]{1,0:T(8,128)(2,1)} %bitcast.170, bf16[16,640]{1,0:T(8,128)(2,1)S(1)} %get-tuple-element.47, bf16[16,640]{1,0:T(8,128)(2,1)S(1)} %get-tuple-element.50), kind=kOutput, calls=%fused_computation.99 | convolution fusion | flops 62996480 | bytes 2203648 | tf_op jit(solution)/shard_map/dot_general | solution.py:118
  48.1 0.5 convolution_add_fusion.1
  48.6 0.5 convolution_add_fusion
  49.1 0.7 pad_maximum_fusion.7
  49.8 3.7 %all-to-all-start.1 = ((bf16[8,8,768]{2,0,1:T(8,128)(2,1)}), bf16[8,8,768]{2,0,1:T(8,128)(2,1)S(1)}, u32[]{:S(2)}, u32[]{:S(2)}) async-start(bf16[8,8,768]{2,0,1:T(8,128)(2,1)} %bitcast.31), calls=%async_computation.1 | async-start | bytes 196608 | tf_op jit(solution)/shard_map/all_to_all | solution.py:125
  53.5 0.1 gt.16
  53.6 5.1 %all-to-all-done.1 = bf16[8,8,768]{2,0,1:T(8,128)(2,1)S(1)} async-done(((bf16[8,8,768]{2,0,1:T(8,128)(2,1)}), bf16[8,8,768]{2,0,1:T(8,128)(2,1)S(1)}, u32[]{:S(2)}, u32[]{:S(2)}) %all-to-all-start.1) | async-done | bytes 98336 | tf_op jit(solution)/shard_map/all_to_all | solution.py:125
  58.8 0.1 stack.96
  58.9 0.7 pad_maximum_fusion.8
  59.6 3.4 %all-to-all-start.2 = ((bf16[8,8,768]{2,1,0:T(8,128)(2,1)}), bf16[8,8,768]{2,1,0:T(8,128)(2,1)S(1)}, u32[]{:S(2)}, u32[]{:S(2)}) async-start(bf16[8,8,768]{2,1,0:T(8,128)(2,1)} %bitcast.40), calls=%async_computation.2 | async-start | bytes 196608 | tf_op jit(solution)/shard_map/all_to_all | solution.py:127
  62.9 5.1 %all-to-all-done.2 = bf16[8,8,768]{2,1,0:T(8,128)(2,1)S(1)} async-done(((bf16[8,8,768]{2,1,0:T(8,128)(2,1)}), bf16[8,8,768]{2,1,0:T(8,128)(2,1)S(1)}, u32[]{:S(2)}, u32[]{:S(2)}) %all-to-all-start.2) | async-done | bytes 98336 | tf_op jit(solution)/shard_map/all_to_all | solution.py:127
  68.2 2.3 %fusion.84 = f32[32,640]{1,0:T(8,128)S(1)} fusion(bf16[32,1536]{1,0:T(8,128)(2,1)S(1)} %bitcast.179, bf16[640,1536]{1,0:T(8,128)(2,1)} %bitcast.172), kind=kOutput, calls=%fused_computation.188 | convolution fusion | flops 62914560 | bytes 2146304 | tf_op jit(solution)/shard_map/dot_general | solution.py:142
  70.6 0.7 fusion.83
  71.2 0.7 fusion.86
  71.9 0.7 fusion.85
  72.7 0.1 squeeze.121
  72.8 0.1 squeeze.59
  72.9 0.1 squeeze.123
  73.0 0.1 squeeze.122
  73.1 0.1 squeeze.120
  73.2 0.1 squeeze.58
  73.3 0.1 neg.40
  73.4 0.1 squeeze.124
  73.6 0.1 fusion.37
  73.7 0.1 copy.53
  73.8 0.1 reshape.914
  73.9 0.7 fusion.15
  74.7 0.9 copy.54
  75.5 0.5 bitcast_bitcast_fusion
  76.0 0.7 reshape.950
  76.7 10.7 %all_to_all.56 = bf16[4,2,5120]{2,1,0:T(2,128)(2,1)S(1)} all-to-all(bf16[4,2,5120]{2,1,0:T(2,128)(2,1)S(1)} %reshape.950), channel_id=1, replica_groups=mesh['wave'=4,'tile'=8] {'wave'}, dimensions={0} | all-to-all | bytes 163840 | tf_op jit(solution)/shard_map/all_to_all | solution.py:160
  87.4 0.5 reshape.951
  87.8 0.9 copy.60
  88.8 0.1 copy.69
  88.9 0.5 copy.58
  89.4 8.3 %convert_bitcast_fusion = bf16[160,2,8,1281]{3,2,1,0:T(8,128)(2,1)} fusion(bf16[160,16,16]{2,1,0:T(8,128)(2,1)S(1)} %copy.58, bf16[160,8,1281]{2,1,0:T(8,128)(2,1)} %get-tuple-element.27, bf16[160,8,1281]{2,1,0:T(8,128)(2,1)} %get-tuple-element.26), kind=kOutput, calls=%fused_computation.5 | convolution fusion | flops 121336320 | bytes 13199360 | tf_op jit(solution)/shard_map/dot_general | solution.py:162
  (49 shorter events, 0.8 us)
Async XLA Ops:
  15.9 26.6 %all-to-all-start = ((bf16[8,2,16,160]{3,2,1,0:T(8,128)(2,1)}), bf16[8,2,16,160]{3,2,1,0:T(8,128)(2,1)S(1)}, u32[]{:S(2)}, u32[]{:S(2)}) async-start(bf16[8,2,16,160]{3,2,1,0:T(8,128)(2,1)} %bitcast.5), calls=%async_computation | async-start | bytes 262144 | tf_op jit(solution)/shard_map/all_to_all | solution.py:101
  39.6 3.0 %copy-start.3 = (s32[640]{0:T(1024)S(1)}, s32[640]{0:T(1024)}, u32[]{:S(2)}) copy-start(s32[640]{0:T(1024)} %param.5) | copy-start | bytes 7684
  43.9 4.2 %copy-start.1 = (bf16[1,20,32,1536]{3,2,1,0:T(8,128)(2,1)S(1)}, bf16[1,20,32,1536]{3,2,1,0:T(8,128)(2,1)}, u32[]{:S(2)}) copy-start(bf16[1,20,32,1536]{3,2,1,0:T(8,128)(2,1)} %get-tuple-element.22) | copy-start | bytes 5898244
  49.8 8.9 %all-to-all-start.1 = ((bf16[8,8,768]{2,0,1:T(8,128)(2,1)}), bf16[8,8,768]{2,0,1:T(8,128)(2,1)S(1)}, u32[]{:S(2)}, u32[]{:S(2)}) async-start(bf16[8,8,768]{2,0,1:T(8,128)(2,1)} %bitcast.31), calls=%async_computation.1 | async-start | bytes 196608 | tf_op jit(solution)/shard_map/all_to_all | solution.py:125
  59.6 8.5 %all-to-all-start.2 = ((bf16[8,8,768]{2,1,0:T(8,128)(2,1)}), bf16[8,8,768]{2,1,0:T(8,128)(2,1)S(1)}, u32[]{:S(2)}, u32[]{:S(2)}) async-start(bf16[8,8,768]{2,1,0:T(8,128)(2,1)} %bitcast.40), calls=%async_computation.2 | async-start | bytes 196608 | tf_op jit(solution)/shard_map/all_to_all | solution.py:127
  68.0 2.5 %copy-start.2 = (bf16[1,20,32,1536]{3,2,1,0:T(8,128)(2,1)S(1)}, bf16[1,20,32,1536]{3,2,1,0:T(8,128)(2,1)}, u32[]{:S(2)}) copy-start(bf16[1,20,32,1536]{3,2,1,0:T(8,128)(2,1)} %get-tuple-element.24) | copy-start | bytes 5898244
  68.1 3.8 %copy-start = (bf16[1,20,32,1536]{3,2,1,0:T(8,128)(2,1)S(1)}, bf16[1,20,32,1536]{3,2,1,0:T(8,128)(2,1)}, u32[]{:S(2)}) copy-start(bf16[1,20,32,1536]{3,2,1,0:T(8,128)(2,1)} %get-tuple-element.25) | copy-start | bytes 5898244
where the time goes:
time: 98.3 us; the launch traced here: 97.7 us
  matrix products  27.7 us (28%)
  other arithmetic  20.9 us (21%)
  starting transfers between devices  13.4 us (14%)
  local copies, waits for them, and re-layouts  11.9 us (12%)
  blocking collectives  10.7 us (11%)
  waiting for transfers between devices  10.2 us (10%)
  between operations  3 us (3%)
    all_to_all x1, blocking collectives, local(): lax.all_to_all(back, 'wave', split_axis=3, concat_axis=0, tiled=True)  10.7 us
    dot_general x1, matrix products, local(): lax.dot_general(masked, spec, (((2,), (2,)), ((0,), (0,))), preferred_ele...  8.57 us
    dot_general x1, matrix products, local(): lax.dot_general(returned, masked, (((2,), (1,)), ((0,), (0,))), preferred...  8.31 us
    cos x2, other arithmetic, trig(): return (jnp.cos(angles), jnp.sin(angles))  7.33 us
    all_to_all x1, starting transfers between devices, local(): lax.all_to_all(coefficients, 'wave', split_axis=0, concat_axis=3, tiled=T...  6.35 us
    all_to_all x1, waiting for transfers between devices, local(): lax.all_to_all(product, 'tile', split_axis=0, concat_axis=1, tiled=True)  5.11 us
    select_n x1, other arithmetic, local(): jnp.where(upper, zero, legendre)  5.11 us
    all_to_all x1, waiting for transfers between devices, local(): lax.all_to_all(grid_values, 'tile', split_axis=1, concat_axis=0, tiled=True)  5.08 us
  transfers between devices with their start and end apart: 3, of which 2 were waited for; matrix products, arithmetic and copies ran while one was open for 18% of the time, Pallas kernels for 0%

commit v1 on v0

--- a/solution.py
+++ b/solution.py
@@ -157,7 +157,19 @@
         back, hot, (((2,), (2,)), ((0,), (0,))), preferred_element_type=F32
     ).astype(BF16)
     back = back.reshape(2, 2, 2 * cols, PAIRS).transpose(1, 0, 2, 3)
-    returned = lax.all_to_all(back, "wave", split_axis=3, concat_axis=0, tiled=True)
+    ways, here = (lax.axis_size("wave"), lax.axis_index("wave"))
+    width = back.shape[3] // ways
+    shape = list(back.shape)
+    shape[3] = width
+    height = shape[0]
+    shape[0] = height * ways
+    full = jnp.zeros(shape, back.dtype)
+    for mask in range(ways):
+        part = lax.dynamic_slice_in_dim(back, (here ^ mask) * width, width, axis=3)
+        if mask:
+            part = lax.ppermute(part, "wave", [(d, d ^ mask) for d in range(ways)])
+        full = lax.dynamic_update_slice_in_dim(full, part, (here ^ mask) * height, axis=0)
+    returned = full
     returned = returned.transpose(3, 2, 1, 0).reshape(slots, 2 * cols, 2 * lat_count)
     result = lax.dot_general(
         returned, masked, (((2,), (1,)), ((0,), (0,))), preferred_element_type=F32

time: 98.3 us -> 95.2 us (0.968)
  blocking collectives: 10.7 us -> 0 us
  waiting for transfers between devices: 10.2 us -> 15.6 us
  starting transfers between devices: 13.4 us -> 18.2 us
  local copies, waits for them, and re-layouts: 11.9 us -> 8.84 us
    all_to_all x1 -> x0, blocking collectives: 10.7 us -> none  [local(): lax.all_to_all(back, 'wave', split_axis=3, concat_axis=0, tiled=True)]
    ppermute x0 -> x3, waiting for transfers between devices: none -> 5.44 us  [local(): part = lax.ppermute(part, 'wave', [(d, d ^ mask) for d in range(ways)])]
    ppermute x0 -> x3, starting transfers between devices: none -> 4.53 us  [local(): part = lax.ppermute(part, 'wave', [(d, d ^ mask) for d in range(ways)])]
    unnamed x12, local copies, waits for them, and re-layouts: 1.62 us -> 0.1 us
  transfers between devices with their start and end apart: 3 -> 6, of which waited for: 2 -> 4; matrix products, arithmetic and copies ran while one was open for 18% -> 19% of each run, Pallas kernels for 0% -> 0%
where the time goes in v1:
time: 95.2 us; the launch traced here: 94.6 us
  matrix products  27.7 us (29%)
  other arithmetic  21 us (22%)
  starting transfers between devices  18.2 us (19%)
  waiting for transfers between devices  15.6 us (16%)
  local copies, waits for them, and re-layouts  8.84 us (9%)
  between operations  3.33 us (3%)
    dot_general x1, matrix products, local(): lax.dot_general(masked, spec, (((2,), (2,)), ((0,), (0,))), preferred_ele...  8.57 us
    dot_general x1, matrix products, local(): lax.dot_general(returned, masked, (((2,), (1,)), ((0,), (0,))), preferred...  8.31 us
    cos x2, other arithmetic, trig(): return (jnp.cos(angles), jnp.sin(angles))  7.33 us
    all_to_all x1, starting transfers between devices, local(): lax.all_to_all(coefficients, 'wave', split_axis=0, concat_axis=3, tiled=T...  6.35 us
    ppermute x3, waiting for transfers between devices, local(): part = lax.ppermute(part, 'wave', [(d, d ^ mask) for d in range(ways)])  5.44 us
    all_to_all x1, waiting for transfers between devices, local(): lax.all_to_all(product, 'tile', split_axis=0, concat_axis=1, tiled=True)  5.11 us
    select_n x1, other arithmetic, local(): jnp.where(upper, zero, legendre)  5.11 us
    all_to_all x1, waiting for transfers between devices, local(): lax.all_to_all(grid_values, 'tile', split_axis=1, concat_axis=0, tiled=True)  5.08 us
  transfers between devices with their start and end apart: 6, of which 4 were waited for; matrix products, arithmetic and copies ran while one was open for 19% of the time, Pallas kernels for 0%

profile of v1, /device:TPU:0, one launch (start us, length us, event | category | flops | bytes accessed | tf_op | source)
XLA Modules:
  0.0 94.6 jit_solution(5233901499985150996)
XLA Ops:
  0.0 0.8 dynamic-slice_subtract_fusion
  0.8 0.2 iota_compare_fusion
  1.0 5.1 %broadcast_select_fusion.1 = (bf16[160,8,1281]{2,1,0:T(8,128)(2,1)}, bf16[160,8,1281]{2,1,0:T(8,128)(2,1)}) fusion(bf16[160,8,1281]{2,1,0:T(8,128)(2,1)} %param.4, pred[160,1281]{1,0:T(8,128)(4,1)S(1)} %iota_compare_fusion), kind=kLoop, calls=%fused_computation.10 | loop fusion | flops 3279360 | bytes 10043040 | tf_op jit(solution)/shard_map/jit(_where)/select_n | solution.py:72
  6.1 8.6 %fusion.12 = bf16[160,2,8,16]{3,2,1,0:T(8,128)(2,1)S(1)} fusion(bf16[160,2,8,1281]{3,2,1,0:T(8,128)(2,1)} %param.3, bf16[160,8,1281]{2,1,0:T(8,128)(2,1)} %get-tuple-element.27, bf16[160,8,1281]{2,1,0:T(8,128)(2,1)} %get-tuple-element.26), kind=kOutput, calls=%fused_computation.19 | convolution fusion | flops 118097920 | bytes 13199360 | tf_op jit(solution)/shard_map/dot_general | solution.py:96
  14.6 1.2 %copy.51 = bf16[160,2,8,16]{0,3,1,2:T(8,128)(2,1)} copy(bf16[160,2,8,16]{3,2,1,0:T(8,128)(2,1)S(1)} %fusion.12) | data formatting | bytes 163840 | tf_op jit(solution)/shard_map/reshape | solution.py:98
  15.9 6.3 %all-to-all-start = ((bf16[8,2,16,160]{3,2,1,0:T(8,128)(2,1)}), bf16[8,2,16,160]{3,2,1,0:T(8,128)(2,1)S(1)}, u32[]{:S(2)}, u32[]{:S(2)}) async-start(bf16[8,2,16,160]{3,2,1,0:T(8,128)(2,1)} %bitcast.5), calls=%async_computation | async-start | bytes 262144 | tf_op jit(solution)/shard_map/all_to_all | solution.py:101
  22.2 0.1 multiply_add_fusion.2
  22.3 0.1 rsqrt_multiply_fusion
  22.4 0.6 fusion.83
  25.9 1.3 %iota_compare_fusion.2 = (pred[1536]{0:T(1024)(128)(4,1)S(1)}, pred[1536]{0:T(1024)(128)(4,1)S(1)}) fusion(s32[]{:T(128)S(6)} %select_n.254, s32[]{:T(128)} %bitcast.2, s32[]{:T(128)} %bitcast.13), kind=kLoop, calls=%fused_computation.140 | loop fusion | flops 7680 | bytes 3084 | tf_op jit(solution)/shard_map/ge | solution.py:84
  27.3 1.3 %compare_select_fusion.1 = (s32[1536]{0:T(1024)S(1)}, f32[1536]{0:T(1024)S(1)}) fusion(s32[]{:T(128)} %bitcast.2, s32[]{:T(128)} %bitcast.13, s32[]{:T(128)S(6)} %select_n.254), kind=kLoop, calls=%fused_computation.127 | loop fusion | flops 7680 | bytes 12300 | tf_op jit(solution)/shard_map/jit(remainder)/jit(_where)/select_n | solution.py:30
  28.6 0.1 fusion.82
  28.7 2.1 %fusion.39 = (f32[20,1536]{1,0:T(8,128)S(1)}, f32[20,1536]{1,0:T(8,128)S(1)}) fusion(f32[1536]{0:T(1024)S(1)} %get-tuple-element.82, pred[1536]{0:T(1024)(128)(4,1)S(1)} %get-tuple-element.84, s32[1536]{0:T(1024)S(1)} %get-tuple-element.81, s32[1536]{0:T(1024)S(1)} %subtract_select_fusion, s32[20]{0:T(128)S(1)} %iota_multiply_fusion), kind=kLoop, calls=%fused_computation.64 | loop fusion | flops 337920 | bytes 265808 | tf_op jit(solution)/shard_map/cos | solution.py:32
  30.8 5.3 %fusion.27 = (f32[2,32,1536]{2,1,0:T(8,128)S(1)}, f32[2,32,1536]{2,1,0:T(8,128)S(1)}) fusion(f32[1536]{0:T(1024)S(1)} %get-tuple-element.82, pred[1536]{0:T(1024)(128)(4,1)S(1)} %get-tuple-element.84, s32[1536]{0:T(1024)S(1)} %get-tuple-element.81, s32[1536]{0:T(1024)S(1)} %subtract_select_fusion, s32[2,32]{1,0:T(2,128)S(1)} %multiply_add_fusion.1), kind=kLoop, calls=%fused_computation.40 | loop fusion | flops 1081344 | bytes 806656 | tf_op jit(solution)/shard_map/cos | solution.py:32
  36.1 2.5 %add_convert_fusion = (bf16[2,20,32,1536]{3,2,1,0:T(8,128)(2,1)S(1)}, bf16[2,20,32,1536]{3,2,1,0:T(8,128)(2,1)S(1)}) fusion(f32[2,32,1536]{2,1,0:T(8,128)S(1)} %get-tuple-element.66, f32[20,1536]{1,0:T(8,128)S(1)} %get-tuple-element.68, f32[2,32,1536]{2,1,0:T(8,128)S(1)} %get-tuple-element.65, f32[20,1536]{1,0:T(8,128)S(1)} %get-tuple-element.67), kind=kLoop, calls=%fused_computation | loop fusion | flops 15728640 | bytes 8896512 | tf_op jit(solution)/shard_map/convert_element_type | solution.py:44
  38.6 1.5 %fusion.76 = (bf16[1,20,32,1536]{3,2,1,0:T(8,128)(2,1)}, bf16[1,20,32,1536]{3,2,1,0:T(8,128)(2,1)S(1)}) fusion(bf16[2,20,32,1536]{3,2,1,0:T(8,128)(2,1)S(1)} %get-tuple-element.28), kind=kLoop, calls=%fused_computation.189 | loop fusion | bytes 7864320 | tf_op jit(solution)/shard_map/slice | solution.py:117
  40.1 2.3 %fusion.77 = (bf16[1,20,32,1536]{3,2,1,0:T(8,128)(2,1)}, bf16[1,20,32,1536]{3,2,1,0:T(8,128)(2,1)}) fusion(bf16[2,20,32,1536]{3,2,1,0:T(8,128)(2,1)S(1)} %get-tuple-element.29), kind=kLoop, calls=%fused_computation.190 | loop fusion | bytes 7864320 | tf_op jit(solution)/shard_map/slice | solution.py:117
  42.4 0.1 compare_select_fusion
  42.5 0.1 broadcast_compare_fusion
  42.6 0.1 mul.344
  42.7 0.1 stack.45
  42.8 0.1 stack.46
  42.9 0.1 copy.84
  43.0 0.1 all_to_all.32
  43.2 0.7 fusion.4
  43.9 0.2 reshape.906
  44.1 0.2 copy.83
  44.2 0.2 reshape.907
  44.5 2.1 %fusion.43 = f32[32,1536]{1,0:T(8,128)S(1)} fusion(bf16[640,1536]{1,0:T(8,128)(2,1)} %bitcast.177, bf16[16,640]{1,0:T(8,128)(2,1)S(1)} %get-tuple-element.43, bf16[16,640]{1,0:T(8,128)(2,1)S(1)} %get-tuple-element.49), kind=kOutput, calls=%fused_computation.91 | convolution fusion | flops 62996480 | bytes 2203648 | tf_op jit(solution)/shard_map/dot_general | solution.py:117
  46.6 2.0 %fusion.50 = f32[32,1536]{1,0:T(8,128)S(1)} fusion(bf16[640,1536]{1,0:T(8,128)(2,1)} %bitcast.173, bf16[16,640]{1,0:T(8,128)(2,1)S(1)} %get-tuple-element.47, bf16[16,640]{1,0:T(8,128)(2,1)S(1)} %get-tuple-element.50), kind=kOutput, calls=%fused_computation.98 | convolution fusion | flops 62996480 | bytes 2203648 | tf_op jit(solution)/shard_map/dot_general | solution.py:118
  48.6 0.5 convolution_add_fusion.1
  49.1 0.5 convolution_add_fusion
  49.6 0.6 pad_maximum_fusion.7
  50.2 3.9 %all-to-all-start.1 = ((bf16[8,8,768]{2,0,1:T(8,128)(2,1)}), bf16[8,8,768]{2,0,1:T(8,128)(2,1)S(1)}, u32[]{:S(2)}, u32[]{:S(2)}) async-start(bf16[8,8,768]{2,0,1:T(8,128)(2,1)} %bitcast.31), calls=%async_computation.1 | async-start | bytes 196608 | tf_op jit(solution)/shard_map/all_to_all | solution.py:125
  54.2 0.1 gt.16
  54.3 5.1 %all-to-all-done.1 = bf16[8,8,768]{2,0,1:T(8,128)(2,1)S(1)} async-done(((bf16[8,8,768]{2,0,1:T(8,128)(2,1)}), bf16[8,8,768]{2,0,1:T(8,128)(2,1)S(1)}, u32[]{:S(2)}, u32[]{:S(2)}) %all-to-all-start.1) | async-done | bytes 98336 | tf_op jit(solution)/shard_map/all_to_all | solution.py:125
  59.5 0.1 stack.96
  59.6 0.6 pad_maximum_fusion.8
  60.2 3.4 %all-to-all-start.2 = ((bf16[8,8,768]{2,1,0:T(8,128)(2,1)}), bf16[8,8,768]{2,1,0:T(8,128)(2,1)S(1)}, u32[]{:S(2)}, u32[]{:S(2)}) async-start(bf16[8,8,768]{2,1,0:T(8,128)(2,1)} %bitcast.40), calls=%async_computation.2 | async-start | bytes 196608 | tf_op jit(solution)/shard_map/all_to_all | solution.py:127
  63.6 5.1 %all-to-all-done.2 = bf16[8,8,768]{2,1,0:T(8,128)(2,1)S(1)} async-done(((bf16[8,8,768]{2,1,0:T(8,128)(2,1)}), bf16[8,8,768]{2,1,0:T(8,128)(2,1)S(1)}, u32[]{:S(2)}, u32[]{:S(2)}) %all-to-all-start.2) | async-done | bytes 98336 | tf_op jit(solution)/shard_map/all_to_all | solution.py:127
  68.9 2.3 %fusion.85 = f32[32,640]{1,0:T(8,128)S(1)} fusion(bf16[32,1536]{1,0:T(8,128)(2,1)S(1)} %bitcast.181, bf16[640,1536]{1,0:T(8,128)(2,1)} %bitcast.175), kind=kOutput, calls=%fused_computation.198 | convolution fusion | flops 62914560 | bytes 2146304 | tf_op jit(solution)/shard_map/dot_general | solution.py:142
  71.2 0.7 fusion.84
  71.9 0.7 fusion.87
  72.6 0.7 fusion.86
  73.4 0.1 squeeze.121
  73.5 0.1 squeeze.59
  73.6 0.1 squeeze.123
  73.7 0.1 squeeze.122
  73.8 0.1 squeeze.120
  73.9 0.1 squeeze.58
  74.0 0.1 neg.40
  74.1 0.1 squeeze.124
  74.3 0.1 fusion.37
  74.4 0.1 copy.60
  74.5 0.1 reshape.914
  74.6 0.7 fusion.15
  75.3 0.1 constant_dynamic-slice_fusion
  75.6 2.1 %collective-permute-start = (bf16[2,2,16,160]{3,0,1,2:T(2,128)(2,1)S(1)}, bf16[2,2,16,160]{3,0,1,2:T(2,128)(2,1)S(1)}, u32[]{:S(2)}, u32[]{:S(2)}) collective-permute-start(bf16[2,2,16,160]{3,0,1,2:T(2,128)(2,1)S(1)} %bitcast.200), channel_id=1, source_target_pairs={{0,8},{8,0},{16,24},{24,16},{1,9},{9,1},{17,25},{25,17},{2,10},{10... | collective-permute-start | bytes 61448 | tf_op jit(solution)/shard_map/ppermute | solution.py:170
  77.7 2.4 %collective-permute-start.1 = (bf16[2,2,16,160]{3,0,1,2:T(2,128)(2,1)S(1)}, bf16[2,2,16,160]{3,0,1,2:T(2,128)(2,1)S(1)}, u32[]{:S(2)}, u32[]{:S(2)}) collective-permute-start(bf16[2,2,16,160]{3,0,1,2:T(2,128)(2,1)S(1)} %bitcast.199), channel_id=1, source_target_pairs={{0,16},{8,24},{16,0},{24,8},{1,17},{9,25},{17,1},{25,9},{2,18},{10... | collective-permute-start | bytes 61448 | tf_op jit(solution)/shard_map/ppermute | solution.py:170
  80.0 0.1 collective-permute-start.2
  80.3 2.4 %collective-permute-done.1 = bf16[2,2,16,160]{3,0,1,2:T(2,128)(2,1)S(1)} collective-permute-done((bf16[2,2,16,160]{3,0,1,2:T(2,128)(2,1)S(1)}, bf16[2,2,16,160]{3,0,1,2:T(2,128)(2,1)S(1)}, u32[]{:S(2)}, u32[]{:S(2)}) %collective-permute-start.1) | collective-permute-done | bytes 20512 | tf_op jit(solution)/shard_map/ppermute | solution.py:170
  82.7 3.0 %collective-permute-done.2 = bf16[2,2,16,160]{3,0,1,2:T(2,128)(2,1)S(1)} collective-permute-done((bf16[2,2,16,160]{3,0,1,2:T(2,128)(2,1)S(1)}, bf16[2,2,16,160]{3,0,1,2:T(2,128)(2,1)S(1)}, u32[]{:S(2)}, u32[]{:S(2)}) %collective-permute-start.2) | collective-permute-done | bytes 20512 | tf_op jit(solution)/shard_map/ppermute | solution.py:170
  85.8 0.5 copy.65
  86.3 8.3 %convert_bitcast_fusion = bf16[160,2,8,1281]{3,2,1,0:T(8,128)(2,1)} fusion(bf16[160,16,16]{2,1,0:T(8,128)(2,1)S(1)} %copy.65, bf16[160,8,1281]{2,1,0:T(8,128)(2,1)} %get-tuple-element.27, bf16[160,8,1281]{2,1,0:T(8,128)(2,1)} %get-tuple-element.26), kind=kOutput, calls=%fused_computation.5 | convolution fusion | flops 121336320 | bytes 13199360 | tf_op jit(solution)/shard_map/dot_general | solution.py:174
  (56 shorter events, 1.0 us)
Async XLA Ops:
  15.9 27.0 %all-to-all-start = ((bf16[8,2,16,160]{3,2,1,0:T(8,128)(2,1)}), bf16[8,2,16,160]{3,2,1,0:T(8,128)(2,1)S(1)}, u32[]{:S(2)}, u32[]{:S(2)}) async-start(bf16[8,2,16,160]{3,2,1,0:T(8,128)(2,1)} %bitcast.5), calls=%async_computation | async-start | bytes 262144 | tf_op jit(solution)/shard_map/all_to_all | solution.py:101
  40.1 3.1 %copy-start.3 = (s32[640]{0:T(1024)S(1)}, s32[640]{0:T(1024)}, u32[]{:S(2)}) copy-start(s32[640]{0:T(1024)} %param.5) | copy-start | bytes 7684
  44.4 4.2 %copy-start.1 = (bf16[1,20,32,1536]{3,2,1,0:T(8,128)(2,1)S(1)}, bf16[1,20,32,1536]{3,2,1,0:T(8,128)(2,1)}, u32[]{:S(2)}) copy-start(bf16[1,20,32,1536]{3,2,1,0:T(8,128)(2,1)} %get-tuple-element.22) | copy-start | bytes 5898244
  50.2 9.1 %all-to-all-start.1 = ((bf16[8,8,768]{2,0,1:T(8,128)(2,1)}), bf16[8,8,768]{2,0,1:T(8,128)(2,1)S(1)}, u32[]{:S(2)}, u32[]{:S(2)}) async-start(bf16[8,8,768]{2,0,1:T(8,128)(2,1)} %bitcast.31), calls=%async_computation.1 | async-start | bytes 196608 | tf_op jit(solution)/shard_map/all_to_all | solution.py:125
  60.2 8.5 %all-to-all-start.2 = ((bf16[8,8,768]{2,1,0:T(8,128)(2,1)}), bf16[8,8,768]{2,1,0:T(8,128)(2,1)S(1)}, u32[]{:S(2)}, u32[]{:S(2)}) async-start(bf16[8,8,768]{2,1,0:T(8,128)(2,1)} %bitcast.40), calls=%async_computation.2 | async-start | bytes 196608 | tf_op jit(solution)/shard_map/all_to_all | solution.py:127
  68.7 2.5 %copy-start.2 = (bf16[1,20,32,1536]{3,2,1,0:T(8,128)(2,1)S(1)}, bf16[1,20,32,1536]{3,2,1,0:T(8,128)(2,1)}, u32[]{:S(2)}) copy-start(bf16[1,20,32,1536]{3,2,1,0:T(8,128)(2,1)} %get-tuple-element.24) | copy-start | bytes 5898244
  68.8 3.8 %copy-start = (bf16[1,20,32,1536]{3,2,1,0:T(8,128)(2,1)S(1)}, bf16[1,20,32,1536]{3,2,1,0:T(8,128)(2,1)}, u32[]{:S(2)}) copy-start(bf16[1,20,32,1536]{3,2,1,0:T(8,128)(2,1)} %get-tuple-element.25) | copy-start | bytes 5898244
  75.6 4.6 %collective-permute-start = (bf16[2,2,16,160]{3,0,1,2:T(2,128)(2,1)S(1)}, bf16[2,2,16,160]{3,0,1,2:T(2,128)(2,1)S(1)}, u32[]{:S(2)}, u32[]{:S(2)}) collective-permute-start(bf16[2,2,16,160]{3,0,1,2:T(2,128)(2,1)S(1)} %bitcast.200), channel_id=1, source_target_pairs={{0,8},{8,0},{16,24},{24,16},{1,9},{9,1},{17,25},{25,17},{2,10},{10... | collective-permute-start | bytes 61448 | tf_op jit(solution)/shard_map/ppermute | solution.py:170
  77.7 5.0 %collective-permute-start.1 = (bf16[2,2,16,160]{3,0,1,2:T(2,128)(2,1)S(1)}, bf16[2,2,16,160]{3,0,1,2:T(2,128)(2,1)S(1)}, u32[]{:S(2)}, u32[]{:S(2)}) collective-permute-start(bf16[2,2,16,160]{3,0,1,2:T(2,128)(2,1)S(1)} %bitcast.199), channel_id=1, source_target_pairs={{0,16},{8,24},{16,0},{24,8},{1,17},{9,25},{17,1},{25,9},{2,18},{10... | collective-permute-start | bytes 61448 | tf_op jit(solution)/shard_map/ppermute | solution.py:170
  80.0 5.7 %collective-permute-start.2 = (bf16[2,2,16,160]{3,0,1,2:T(2,128)(2,1)S(1)}, bf16[2,2,16,160]{3,0,1,2:T(2,128)(2,1)S(1)}, u32[]{:S(2)}, u32[]{:S(2)}) collective-permute-start(bf16[2,2,16,160]{3,0,1,2:T(2,128)(2,1)S(1)} %bitcast.198), channel_id=1, source_target_pairs={{0,24},{8,16},{16,8},{24,0},{1,25},{9,17},{17,9},{25,1},{2,26},{10... | collective-permute-start | bytes 61448 | tf_op jit(solution)/shard_map/ppermute | solution.py:170
